TPU v7x, 32 devices: a whole 2x2x4 slice. The times are simulated.
32 devices in a mesh: dp: 4 (over y, x), seq: 8 (over z, core).
Axes of the slice: x: 2, y: 2, z: 4, core: 2. Of those that a mesh axis runs over, the one named last changes fastest.
Arguments:
- section_input: bfloat16 [16384, 1536], P(('dp', 'seq')), parts along dimension 0, may hold values from -6 to 6
- conv_gain: float32 [1536], replicated, may hold values from 0.1 to 1.9
- conv_weight: bfloat16 [5, 1536, 1536], replicated, may hold values from -0.0625 to 0.0625
- conv_bias: float32 [1536], replicated, may hold values from -3 to 3
- attn_gain: float32 [1536], replicated, may hold values from 0.1 to 1.9
- q_weight: bfloat16 [1536, 1024], P('seq'), may hold values from -5 to 5
- kv_weight: bfloat16 [1536, 320], P('seq'), may hold values from -0.15625 to 0.15625
- o_weight: bfloat16 [1536, 1536], P('seq'), may hold values from -0.15625 to 0.15625
Outputs:
- skip: bfloat16 [8192, 1536], P(('dp', 'seq')), parts along dimension 0
- block_out: bfloat16 [8192, 1536], P(('dp', 'seq')), parts along dimension 0
There are 4 independent parts, one for each index of `dp`. A program takes and returns all parts, laid end to end along the dimension named above; an argument that names none is the same for every part. Nothing has to cross between parts.
All inputs are finite; a program needn't handle non-finite values.
Results may differ from a plain program's by a relative error of at most 0.008.
The roundings to bfloat16 on the way count: a program that leaves them out, or rounds other values in their place, can miss the bound.
Values may be sent and summed in bfloat16 or wider, within the bound.
A program may use at most 192 MiB of HBM per device.

v0:
```python
import jax
import jax.numpy as jnp
from jax import lax
from jax.sharding import PartitionSpec as P

HEADS = 8
DK = 128


def padded_2(array, sides, width):
    for axis, dim in sides:
        count, length = (lax.axis_size(axis), array.shape[dim])
        up = [(i, (i + 1) % count) for i in range(count - 1)]
        down = [(j, i) for i, j in up]
        last = lax.slice_in_dim(array, length - width, length, axis=dim)
        initial = lax.slice_in_dim(array, 0, width, axis=dim)
        before = lax.ppermute(last, axis, up)
        after = lax.ppermute(initial, axis, down)
        array = jnp.concatenate([before, array, after], axis=dim)
    return array


def rms_scale(rows, gain):
    values = rows.astype(jnp.float32)
    return values * lax.rsqrt(jnp.mean(values * values, axis=-1, keepdims=True) + 1e-06) * gain


def rotate(values, positions):
    half_size = values.shape[-1] // 2
    freqs = jnp.power(10000.0, -jnp.arange(half_size, dtype=jnp.float32) / half_size)
    angle = positions.astype(jnp.float32)[:, None] * freqs[None, :]
    if values.ndim == 3:
        angle = angle[:, None, :]
    cosine = jnp.cos(angle)
    sine = jnp.sin(angle)
    first = values[..., :half_size]
    second = values[..., half_size:]
    return jnp.concatenate(
        [first * cosine - second * sine, second * cosine + first * sine], axis=-1
    )


def activate(rows, gain):
    return jax.nn.gelu(rms_scale(rows, gain), approximate=True).astype(jnp.bfloat16)


def body(
    section_input, conv_gain, conv_weight, conv_bias, attn_gain, q_weight, kv_weight, o_weight
):
    pos_rows, width = section_input.shape
    tok_rows = pos_rows // 2
    taps = conv_weight.shape[0]
    reach = taps // 2
    key_size = kv_weight.shape[1] - o_weight.shape[0] // 1 * 0
    head_count = HEADS
    key_size = DK
    activated = activate(section_input, conv_gain)
    padded = padded_2(activated, (("seq", 0),), reach)
    conv = jnp.zeros((pos_rows, width), jnp.float32) + conv_bias
    for kernel_tap in range(taps):
        conv = conv + jnp.dot(
            padded[kernel_tap : kernel_tap + pos_rows],
            conv_weight[kernel_tap],
            preferred_element_type=jnp.float32,
        )
    summed = section_input.astype(jnp.float32) + conv
    skip = jnp.max(summed.reshape(tok_rows, 2, width), axis=1).astype(jnp.bfloat16)
    normed = rms_scale(skip, attn_gain).astype(jnp.bfloat16)
    slab_rows = (
        lax.all_gather(q_weight, "seq", axis=0, tiled=True),
        lax.all_gather(kv_weight, "seq", axis=0, tiled=True),
    )
    columns = normed
    query_sums = jnp.dot(columns, slab_rows[0], preferred_element_type=jnp.float32)
    projected = jnp.dot(columns, slab_rows[1], preferred_element_type=jnp.float32)
    positions = lax.axis_index("seq") * tok_rows + jnp.arange(tok_rows, dtype=jnp.int32)
    queries = rotate(query_sums.reshape(tok_rows, head_count, key_size), positions).astype(
        jnp.bfloat16
    )
    keys = rotate(projected[:, :key_size], positions)
    key_values = jnp.concatenate([keys, projected[:, key_size:]], axis=1).astype(jnp.bfloat16)
    score_scale = key_size ** (-0.5)
    value_size = key_values.shape[1] - key_size
    slab_rows = lax.all_gather(key_values, "seq", axis=0, tiled=True)
    peak_old = jnp.full((head_count, tok_rows), -1e30, jnp.float32)
    slab_keys = slab_rows[:, :key_size]
    slab_values = slab_rows[:, key_size:]
    scores = (
        jnp.einsum("thd,kd->htk", queries, slab_keys, preferred_element_type=jnp.float32)
        * score_scale
    )
    peak_new = jnp.maximum(peak_old, jnp.max(scores, axis=-1))
    weights = jnp.exp(scores - peak_new[..., None])
    total_new = jnp.sum(weights, axis=-1)
    summed_new = jnp.einsum(
        "htk,kv->htv", weights.astype(jnp.bfloat16), slab_values, preferred_element_type=jnp.float32
    )
    heads_out = summed_new / total_new[..., None]
    mixed = (
        jnp.transpose(heads_out, (1, 0, 2))
        .reshape(tok_rows, head_count * value_size)
        .astype(jnp.bfloat16)
    )
    columns = mixed
    attended = jnp.dot(
        columns,
        lax.all_gather(o_weight, "seq", axis=0, tiled=True),
        preferred_element_type=jnp.float32,
    )
    block_out = (skip.astype(jnp.float32) + attended).astype(jnp.bfloat16)
    return (skip, block_out)


def solution(mesh):
    in_specs = (
        P(("dp", "seq"), None),
        P(),
        P(),
        P(),
        P(),
        P("seq", None),
        P("seq", None),
        P("seq", None),
    )
    out_specs = (P(("dp", "seq"), None), P(("dp", "seq"), None))
    return jax.shard_map(body, mesh=mesh, in_specs=in_specs, out_specs=out_specs, check_vma=False)
```

profile of v0, /device:TPU:17, one launch (start us, length us, event | category | flops | bytes accessed | tf_op | source)
XLA Modules:
  0.0 158.4 jit_solution(12263147461915845566)
XLA Ops:
  7.2 0.0 copy-start.4
  7.2 0.0 all-gather.6.cloned.1.call-start
  7.2 1.8 %fusion.37 = f32[512]{0:T(512)S(1)} fusion(bf16[512,1536]{1,0:T(8,128)(2,1)} %param.8), kind=kLoop, calls=%fused_computation.32 | loop fusion | flops 2358784 | bytes 1574912 | tf_op jit(solution)/shard_map/reduce_sum | solution.py:25
  9.0 2.8 %fusion.41 = bf16[512,1536]{1,0:T(8,128)(2,1)S(1)} fusion(bf16[512,1536]{1,0:T(8,128)(2,1)} %param.8, f32[1536]{0:T(1024)} %param.9, f32[512]{0:T(512)S(1)} %add_rsqrt_fusion), kind=kLoop, calls=%fused_computation.36 | loop fusion | flops 9437184 | bytes 3153920 | tf_op jit(solution)/shard_map/convert_element_type | solution.py:44
  11.9 3.8 %collective-permute-start = (bf16[2,1536]{1,0:T(2,128)(2,1)S(1)}, bf16[2,1536]{1,0:T(2,128)(2,1)S(1)}, u32[]{:S(2)}, u32[]{:S(2)}) collective-permute-start(bf16[2,1536]{1,0:T(2,128)(2,1)S(1)} %get-tuple-element.4), channel_id=1, source_target_pairs={{0,1},{1,2},{2,3},{3,4},{4,5},{5,6},{6,7},{8,9},{9,10},{10,11},{11... | collective-permute-start | bytes 18440 | tf_op jit(solution)/shard_map/ppermute | solution.py:17
  15.6 1.9 %collective-permute-start.1 = (bf16[2,1536]{1,0:T(2,128)(2,1)S(1)}, bf16[2,1536]{1,0:T(2,128)(2,1)S(1)}, u32[]{:S(2)}, u32[]{:S(2)}) collective-permute-start(bf16[2,1536]{1,0:T(2,128)(2,1)S(1)} %get-tuple-element.5), channel_id=1, source_target_pairs={{1,0},{2,1},{3,2},{4,3},{5,4},{6,5},{7,6},{9,8},{10,9},{11,10},{12... | collective-permute-start | bytes 18440 | tf_op jit(solution)/shard_map/ppermute | solution.py:18
  17.6 0.0 all-gather.6.cloned.1.call-update
  17.6 0.0 all-gather.4.cloned.1.call-start
  17.7 0.0 copy-done.4
  17.7 20.2 %all_gather.12 = bf16[1536,320]{1,0:T(8,128)(2,1)} all-gather(bf16[192,320]{1,0:T(8,128)(2,1)S(1)} %copy-done.4), channel_id=1, replica_groups=mesh['dp'=4,'seq'=8] {'seq'}, dimensions={0}, use_global_device_ids=true | all-gather | bytes 1105920 | tf_op jit(solution)/shard_map/all_gather | solution.py:71
  37.9 4.5 %fusion.11 = f32[512,1536]{1,0:T(8,128)S(1)} fusion(bf16[512,1536]{1,0:T(8,128)(2,1)S(1)} %fusion.41, bf16[5,1536,1536]{2,1,0:T(8,128)(2,1)} %param.10), kind=kOutput, calls=%fused_computation.16 | convolution fusion | flops 2415919104 | bytes 9437184 | tf_op jit(solution)/shard_map/dot_general | solution.py:61
  42.4 0.0 collective-permute-done
  42.4 4.5 %fusion.13 = f32[512,1536]{1,0:T(8,128)S(1)} fusion(bf16[5,1536,1536]{2,1,0:T(8,128)(2,1)} %param.10, bf16[512,1536]{1,0:T(8,128)(2,1)S(1)} %fusion.41, bf16[2,1536]{1,0:T(2,128)(2,1)S(1)} %collective-permute-done), kind=kOutput, calls=%fused_computation.18 | convolution fusion | flops 2419064832 | bytes 9443328 | tf_op jit(solution)/shard_map/dot_general | solution.py:61
  46.9 0.0 collective-permute-done.1
  46.9 4.6 %fusion.7 = f32[512,1536]{1,0:T(8,128)S(1)} fusion(bf16[5,1536,1536]{2,1,0:T(8,128)(2,1)} %param.10, bf16[2,1536]{1,0:T(2,128)(2,1)S(1)} %collective-permute-done.1, bf16[512,1536]{1,0:T(8,128)(2,1)S(1)} %fusion.41), kind=kOutput, calls=%fused_computation.12 | convolution fusion | flops 2419064832 | bytes 9443328 | tf_op jit(solution)/shard_map/dot_general | solution.py:61
  51.6 0.0 copy-start
  51.6 0.0 copy-start.5
  51.6 4.7 %fusion.9 = f32[512,1536]{1,0:T(8,128)S(1)} fusion(bf16[5,1536,1536]{2,1,0:T(8,128)(2,1)} %param.10, bf16[512,1536]{1,0:T(8,128)(2,1)S(1)} %fusion.41, bf16[2,1536]{1,0:T(2,128)(2,1)S(1)} %collective-permute-done.1), kind=kOutput, calls=%fused_computation.14 | convolution fusion | flops 2419064832 | bytes 9443328 | tf_op jit(solution)/shard_map/dot_general | solution.py:61
  56.3 0.0 copy-done
  56.4 0.0 copy-done.5
  56.4 5.3 %convert_add_fusion = bf16[512,1536]{1,0:T(8,128)(2,1)S(1)} fusion(bf16[512,1536]{1,0:T(8,128)(2,1)S(1)} %copy-done, f32[512,1536]{1,0:T(8,128)S(1)} %fusion.7, f32[512,1536]{1,0:T(8,128)S(1)} %fusion.9, f32[512,1536]{1,0:T(8,128)S(1)} %fusion.11, f32[512,1536]{1,0:T(8,128)S(1)} %fusion.13, bf16[5,1536,1536]{2,1,0:T(8,128)(2,1)} %param.10, ...), kind=kOutput, calls=%fused_computation.9 | convolution fusion | flops 2425356288 | bytes 22032384 | tf_op jit(solution)/shard_map/dot_general | solution.py:61
  61.7 0.0 copy-start.6
  61.7 0.8 reshape.95
  62.5 0.0 copy-start.2
  62.5 4.3 %reduce_max.18 = bf16[256,1536]{1,0:T(8,128)(2,1)S(1)} reduce(bf16[256,2,1536]{2,1,0:T(2,128)(2,1)S(1)} %reshape.95, bf16[]{:T(256)} %constant.113), dimensions={1}, to_apply=%region_1.0 | reduce | flops 393216 | bytes 2359298 | tf_op jit(solution)/shard_map/reduce_max | solution.py:67
  66.8 0.0 copy-start.1
  66.8 0.2 fusion.54
  67.1 0.0 copy-done.6
  67.1 0.0 copy-done.2
  67.1 0.6 fusion.67
  67.8 0.3 multiply_cosine_fusion
  68.1 0.7 pad_maximum_fusion.4
  68.8 0.0 all-gather.4.cloned.1.call-update
  68.8 0.0 all-gather.8.cloned.1.call-start
  68.8 0.7 all-gather.8.cloned.1.call-update
  69.5 0.1 copy.11
  69.6 0.1 copy.13
  69.7 0.0 all-gather.6.cloned.1.call-done
  69.8 2.9 %convolution_bitcast_fusion = f32[32,8,8,128]{3,1,2,0:T(8,128)S(1)} fusion(bf16[1536,1024]{1,0:T(8,128)(2,1)} %all-gather.6.cloned.1.call-done, bf16[256,1536]{1,0:T(8,128)(2,1)S(1)} %reduce_max.18, f32[1536]{0:T(1024)S(1)} %copy-done.6, f32[256]{0:T(256)S(1)} %add_rsqrt_fusion.1), kind=kOutput, calls=%fused_computation.61 | convolution fusion | flops 806879232 | bytes 4987904 | tf_op jit(solution)/shard_map/dot_general | solution.py:74
  72.7 0.2 copy.21
  72.9 0.3 fusion.76
  73.2 0.4 subtract_convert_fusion
  73.6 20.8 %all-gather.4.cloned.1.call-done = bf16[2048,320]{0,1:T(8,128)(2,1)} async-done(((bf16[256,320]{0,1:T(8,128)(2,1)}), bf16[2048,320]{0,1:T(8,128)(2,1)}) %all-gather.4.cloned.1.call-update) | async-done | bytes 1310736 | tf_op jit(solution)/shard_map/all_gather | solution.py:84
  94.5 8.1 %bitcast_reduce_fusion = (f32[8,256]{1,0:T(8,128)S(1)}, f32[2048,256,8]{1,0,2:T(8,128)}) fusion(bf16[256,8,64]{2,0,1:T(8,128)(2,1)S(1)} %get-tuple-element.3, bf16[256,8,64]{2,0,1:T(8,128)(2,1)S(1)} %get-tuple-element.2, bf16[2048,320]{0,1:T(8,128)(2,1)} %all-gather.4.cloned.1.call-done), kind=kOutput, calls=%fused_computation.1 | convolution fusion | flops 1083176960 | bytes 17833984 | tf_op jit(solution)/shard_map/thd,kd->htk/dot_general | solution.py:89
  102.6 9.5 %fusion.1 = f32[8,256]{1,0:T(8,128)S(1)} fusion(f32[2048,256,8]{1,0,2:T(8,128)} %get-tuple-element.15, f32[8,256]{1,0:T(8,128)S(1)} %broadcast_maximum_fusion), kind=kLoop, calls=%fused_computation.3 | loop fusion | flops 12580864 | bytes 16793600 | tf_op jit(solution)/shard_map/reduce_sum | solution.py:94
  112.1 9.1 %fusion.59 = bf16[256,8,192]{0,2,1:T(8,128)(2,1)S(1)} fusion(f32[2048,256,8]{1,0,2:T(8,128)} %get-tuple-element.15, f32[8,256]{1,0:T(8,128)S(1)} %broadcast_maximum_fusion, bf16[2048,320]{0,1:T(8,128)(2,1)S(1)} %copy-done.3, f32[256,8]{0,1:T(8,128)S(1)} %bitcast.62), kind=kOutput, calls=%fused_computation.60 | convolution fusion | flops 1623982080 | bytes 18366464 | tf_op jit(solution)/shard_map/htk,kv->htv/dot_general | solution.py:95
  121.2 26.0 %all-gather.8.cloned.1.call-done = bf16[1536,1536]{1,0:T(8,128)(2,1)} async-done(((bf16[192,1536]{1,0:T(8,128)(2,1)}), bf16[1536,1536]{1,0:T(8,128)(2,1)}) %all-gather.8.cloned.1.call-update) | async-done | bytes 4718608 | tf_op jit(solution)/shard_map/all_gather | solution.py:107
  147.2 4.6 %fusion.49 = bf16[256,1536]{1,0:T(8,128)(2,1)} fusion(bf16[256,1536]{0,1:T(8,128)(2,1)S(1)} %bitcast.63, bf16[1536,1536]{1,0:T(8,128)(2,1)} %all-gather.8.cloned.1.call-done, bf16[256,1536]{1,0:T(8,128)(2,1)S(1)} %reduce_max.18), kind=kOutput, calls=%fused_computation.43 | convolution fusion | flops 1209139200 | bytes 7077888 | tf_op jit(solution)/shard_map/dot_general | solution.py:105
  (10 shorter events, 0.1 us)
Async XLA Ops:
  7.2 10.5 %copy-start.4 = (bf16[192,320]{1,0:T(8,128)(2,1)S(1)}, bf16[192,320]{1,0:T(8,128)(2,1)}, u32[]{:S(2)}) copy-start(bf16[192,320]{1,0:T(8,128)(2,1)} %param.14) | copy-start | bytes 368644
  7.2 62.6 %all-gather.6.cloned.1.call-start = ((), (), s32[]{:S(2)}) async-start(), calls=%async_computation.1 | async-start | bytes 3538944 | tf_op jit(solution)/shard_map/all_gather | solution.py:70
  11.9 30.5 %collective-permute-start = (bf16[2,1536]{1,0:T(2,128)(2,1)S(1)}, bf16[2,1536]{1,0:T(2,128)(2,1)S(1)}, u32[]{:S(2)}, u32[]{:S(2)}) collective-permute-start(bf16[2,1536]{1,0:T(2,128)(2,1)S(1)} %get-tuple-element.4), channel_id=1, source_target_pairs={{0,1},{1,2},{2,3},{3,4},{4,5},{5,6},{6,7},{8,9},{9,10},{10,11},{11... | collective-permute-start | bytes 18440 | tf_op jit(solution)/shard_map/ppermute | solution.py:17
  15.6 31.3 %collective-permute-start.1 = (bf16[2,1536]{1,0:T(2,128)(2,1)S(1)}, bf16[2,1536]{1,0:T(2,128)(2,1)S(1)}, u32[]{:S(2)}, u32[]{:S(2)}) collective-permute-start(bf16[2,1536]{1,0:T(2,128)(2,1)S(1)} %get-tuple-element.5), channel_id=1, source_target_pairs={{1,0},{2,1},{3,2},{4,3},{5,4},{6,5},{7,6},{9,8},{10,9},{11,10},{12... | collective-permute-start | bytes 18440 | tf_op jit(solution)/shard_map/ppermute | solution.py:18
  17.6 76.9 %all-gather.4.cloned.1.call-start = ((), (), s32[]{:S(2)}) async-start(), calls=%async_computation | async-start | bytes 1474560 | tf_op jit(solution)/shard_map/all_gather | solution.py:84
  51.6 4.8 %copy-start = (bf16[512,1536]{1,0:T(8,128)(2,1)S(1)}, bf16[512,1536]{1,0:T(8,128)(2,1)}, u32[]{:S(2)}) copy-start(bf16[512,1536]{1,0:T(8,128)(2,1)} %param.8) | copy-start | bytes 4718596
  51.6 4.8 %copy-start.5 = (f32[1536]{0:T(1024)S(1)}, f32[1536]{0:T(1024)}, u32[]{:S(2)}) copy-start(f32[1536]{0:T(1024)} %param.11) | copy-start | bytes 18436
  61.7 5.4 %copy-start.6 = (f32[1536]{0:T(1024)S(1)}, f32[1536]{0:T(1024)}, u32[]{:S(2)}) copy-start(f32[1536]{0:T(1024)} %param.12) | copy-start | bytes 18436
  62.5 4.6 %copy-start.2 = (bf16[1536,320]{1,0:T(8,128)(2,1)S(1)}, bf16[1536,320]{1,0:T(8,128)(2,1)}, u32[]{:S(2)}) copy-start(bf16[1536,320]{1,0:T(8,128)(2,1)} %all_gather.12) | copy-start | bytes 2949124
  66.8 80.4 %copy-start.1 = (bf16[256,1536]{1,0:T(8,128)(2,1)}, bf16[256,1536]{1,0:T(8,128)(2,1)S(1)}, u32[]{:S(2)}) copy-start(bf16[256,1536]{1,0:T(8,128)(2,1)S(1)} %reduce_max.18) | copy-start | bytes 2359300
  68.8 78.4 %all-gather.8.cloned.1.call-start = ((), (), s32[]{:S(2)}) async-start(), calls=%async_computation.2 | async-start | bytes 5308416 | tf_op jit(solution)/shard_map/all_gather | solution.py:107
  102.6 9.5 %copy-start.3 = (bf16[2048,320]{0,1:T(8,128)(2,1)S(1)}, bf16[2048,320]{0,1:T(8,128)(2,1)}, u32[]{:S(2)}) copy-start(bf16[2048,320]{0,1:T(8,128)(2,1)} %all-gather.4.cloned.1.call-done) | copy-start | bytes 3932164
Sparse Core Ops, SparseCore 0:
  17.7 41.8 all-gather.5
  68.9 25.5 all-gather.3
  96.1 51.0 all-gather.7
where the time goes:
time: 161 us; the launch traced here: 158 us
  matrix products  49.1 us (30%)
  waiting for transfers between devices  47.6 us (30%)
  blocking collectives  20.2 us (13%)
  other arithmetic  20 us (12%)
  between operations  14 us (9%)
  starting transfers between devices  5.81 us (4%)
    all_gather x1, waiting for transfers between devices, body(): lax.all_gather(o_weight, 'seq', axis=0, tiled=True)  26 us
    dot_general x5, matrix products, body(): jnp.dot(padded[kernel_tap:kernel_tap + pos_rows], conv_weight[kernel_tap]...  23.6 us
    all_gather x1, waiting for transfers between devices, body(): slab_rows = lax.all_gather(key_values, 'seq', axis=0, tiled=True)  20.8 us
    all_gather x1, blocking collectives, body(): lax.all_gather(kv_weight, 'seq', axis=0, tiled=True)  20.2 us
    reduce_sum x1, other arithmetic, body(): total_new = jnp.sum(weights, axis=-1)  9.45 us
    dot_general x1, matrix products, body(): jnp.einsum('htk,kv->htv', weights.astype(jnp.bfloat16), slab_values, pref...  9.14 us
    dot_general x1, matrix products, body(): jnp.einsum('thd,kd->htk', queries, slab_keys, preferred_element_type=jnp....  8.13 us
    dot_general x1, matrix products, body(): jnp.dot(columns, lax.all_gather(o_weight, 'seq', axis=0, tiled=True), pre...  4.62 us
  transfers between devices with their start and end apart: 5, of which 2 were waited for; matrix products, arithmetic and copies ran while one was open for 39% of the time, Pallas kernels for 0%

commit v1 on v0

v1 whole, which is shorter than its diff:
```python
import functools

import jax
import jax.numpy as jnp
from jax import lax
from jax.experimental import pallas as pl
from jax.experimental.pallas import tpu as pltpu
from jax.sharding import PartitionSpec as P

HEADS = 8
DK = 128
TILE = 256
F32 = jnp.float32
BF16 = jnp.bfloat16
MESH = pl.DeviceIdType.MESH


def pieces_of(dp, rows):
    for g in (4, 2):
        if dp % g == 0 and rows % (16 * g) == 0:
            return g
    return 1


def kernel(
    cfg, x_hbm, cgain, cw_hbm, cbias, again, q_hbm, kv_hbm, o_hbm, cs_ref,
    skip_hbm, out_hbm,
    xin, halo, resid, pad, stack, cw, acc, skip, normed, wq, wkv, wo, own, kvbuf, queries,
    peak, attn, mixed, outv,
    in_sem, cw_sem, loc_sem, halo_s, halo_r, p1_s, p1_r, p2_s, p2_r, p3_s, p3_r, p4_s, p4_r,
    kd_s, kd_r, kp_s, kp_r, out_sem,
):
    D, S, G, R = cfg
    Z = S // 2
    rows, width = xin.shape
    toks = rows // 2
    n_tiles = width // TILE
    taps = cw.shape[1]
    dv = kv_hbm.shape[1] - DK
    d = lax.axis_index("dp")
    s = lax.axis_index("seq")
    c = lax.rem(s, 2)
    z = s // 2
    partner = s + 1 - 2 * c
    rp = R // G
    me = d % G
    if G == 4:
        f1 = d + 1 - 2 * (d % 2)
        f2 = d + 2 - 4 * ((d // 2) % 2)
        ax1 = f1 + c * (f2 - f1)
        ax2 = f2 + c * (f1 - f2)
    elif G == 2:
        ax1 = d + 1 - 2 * (d % 2)
        ax2 = None
    else:
        ax1 = ax2 = None

    up = (s + 1) % S
    down = (s + S - 1) % S

    def fwd(k):
        return ((z + k) % Z) * 2 + c

    def src(k):
        return ((z + Z - k) % Z) * 2 + c

    in_copy = pltpu.make_async_copy(x_hbm, xin, in_sem)
    in_copy.start()
    cw_copies = []
    for n in range(n_tiles):
        cp = pltpu.make_async_copy(
            cw_hbm.at[:, :, pl.ds(n * TILE, TILE)], cw.at[n], cw_sem.at[n]
        )
        cp.start()
        cw_copies.append(cp)

    greet = [(d, up), (d, down), (d, partner)] + [(d, fwd(k)) for k in range(1, Z)]
    if ax1 is not None:
        greet.append((ax1, s))
    if ax2 is not None:
        greet.append((ax2, s))
    bar = pltpu.get_barrier_semaphore()
    for g in greet:
        pl.semaphore_signal(bar, inc=1, device_id=g, device_id_type=MESH)
    pl.semaphore_wait(bar, len(greet))

    def remote(a, b, ss, rs, dev):
        return pltpu.make_async_remote_copy(
            src_ref=a, dst_ref=b, send_sem=ss, recv_sem=rs, device_id=dev, device_id_type=MESH
        )

    sent = []

    def start(cp):
        cp.start()
        sent.append(cp)
        return cp

    h_up = start(remote(x_hbm.at[pl.ds(rows - 16, 16)], halo.at[0], halo_s.at[0], halo_r.at[0], (d, up)))
    h_dn = start(remote(x_hbm.at[pl.ds(0, 16)], halo.at[1], halo_s.at[1], halo_r.at[1], (d, down)))

    hbms = (kv_hbm, q_hbm, o_hbm)
    bufs = (wkv, wq, wo)

    def al(v, m):
        return pl.multiple_of(v, m)

    ph1, ph2, ph3, ph4, locs = {}, {}, {}, {}, {}

    def phase1(a):
        for k in range(1, Z):
            at = pl.ds(al(me * rp, 16), rp)
            to = pl.ds(al(s * R + me * rp, 16), rp)
            ph1[a, k] = start(remote(
                hbms[a].at[at], bufs[a].at[to], p1_s.at[a, k - 1], p1_r.at[a, k - 1], (d, fwd(k))
            ))
        whole = pl.ds(al(s * R, 16), R)
        ph4[a, 0] = start(remote(
            hbms[a], bufs[a].at[whole], p4_s.at[a, 0], p4_r.at[a, 0], (d, partner)
        ))
        locs[a] = pltpu.make_async_copy(hbms[a], bufs[a].at[whole], loc_sem.at[a])
        locs[a].start()

    def phase2(a):
        for k in range(1, Z):
            ph1[a, k].wait_recv()
            if ax1 is not None:
                at = bufs[a].at[pl.ds(al(src(k) * R + me * rp, 16), rp)]
                ph2[a, k] = start(remote(at, at, p2_s.at[a, k - 1], p2_r.at[a, k - 1], (ax1, s)))

    def phase3(a):
        for k in range(1, Z):
            if ax1 is not None:
                ph2[a, k].wait_recv()
            if ax2 is not None:
                for i, piece in enumerate((me, ax1 % G)):
                    at = bufs[a].at[pl.ds(al(src(k) * R + piece * rp, 16), rp)]
                    ph3[a, k, i] = start(remote(
                        at, at, p3_s.at[a, k - 1, i], p3_r.at[a, k - 1, i], (ax2, s)
                    ))

    def phase4(a):
        for k in range(1, Z):
            if ax2 is not None:
                ph3[a, k, 0].wait_recv()
                ph3[a, k, 1].wait_recv()
            at = bufs[a].at[pl.ds(al(src(k) * R, 16), R)]
            ph4[a, k] = start(remote(at, at, p4_s.at[a, k], p4_r.at[a, k], (d, partner)))

    def ready(a):
        locs[a].wait()
        for k in range(Z):
            ph4[a, k].wait_recv()

    phase1(0)
    phase1(1)

    def act(v):
        scale = lax.rsqrt(jnp.mean(v * v, axis=-1, keepdims=True) + 1e-06)
        return jax.nn.gelu(v * scale * cgain[...], approximate=True)

    in_copy.wait()
    step_rows = 16

    def act_rows(i, carry):
        at = al(i * step_rows, step_rows)
        v = xin[pl.ds(at, step_rows), :].astype(F32)
        a = act(v)
        for j in range(width // 128):
            resid[j, pl.ds(at, step_rows), :] = v[:, j * 128:(j + 1) * 128]
            pad[j, pl.ds(al(8 + i * step_rows, 8), step_rows), :] = a[:, j * 128:(j + 1) * 128]
        return carry

    lax.fori_loop(0, rows // step_rows, act_rows, 0)
    h_up.wait_recv()
    h_dn.wait_recv()
    before = act(halo[0].astype(F32))[8:16, :] * jnp.where(s > 0, 1.0, 0.0).astype(F32)
    after = act(halo[1].astype(F32))[0:8, :] * jnp.where(s < S - 1, 1.0, 0.0).astype(F32)
    for j in range(width // 128):
        cols = slice(j * 128, (j + 1) * 128)
        pad[j, 0:8, :] = before[:, cols]
        pad[j, rows + 8:rows + 16, :] = after[:, cols]
        for b in range(taps + 1):
            stack[b * toks:(b + 1) * toks, cols] = pad[
                j, pl.ds(6 + b, toks, stride=2), :
            ].astype(BF16)

    events = {1: (lambda: phase2(0), lambda: phase2(1), lambda: phase1(2)),
              3: (lambda: phase3(0), lambda: phase3(1)),
              4: (lambda: phase4(0), lambda: phase4(1))}
    for n in range(n_tiles):
        cw_copies[n].wait()
        acc[...] = jnp.broadcast_to(cbias[:, n * TILE:(n + 1) * TILE], acc.shape)

        def tap(t, carry):
            acc[...] += jnp.dot(
                stack[pl.ds(al(t * toks, 16), 2 * toks), :], cw[n, t], preferred_element_type=F32
            )
            return carry

        lax.fori_loop(0, taps, tap, 0)
        for i in range(TILE // 128):
            j = n * TILE // 128 + i
            part = slice(i * 128, (i + 1) * 128)
            even = resid[j, pl.ds(0, toks, stride=2), :] + acc[0:toks, part]
            odd = resid[j, pl.ds(1, toks, stride=2), :] + acc[toks:2 * toks, part]
            skip[:, j * 128:(j + 1) * 128] = jnp.maximum(even, odd).astype(BF16)
        for e in events.get(n, ()):
            e()

    skip_out = pltpu.make_async_copy(skip, skip_hbm, out_sem.at[0])
    skip_out.start()

    def norm_rows(i, carry):
        at = pl.ds(al(i * 16, 16), 16)
        v = skip[at, :].astype(F32)
        scale = lax.rsqrt(jnp.mean(v * v, axis=-1, keepdims=True) + 1e-06)
        normed[at, :] = (v * scale * again[...]).astype(BF16)
        return carry

    lax.fori_loop(0, toks // 16, norm_rows, 0)

    cosine = cs_ref[:, 0:DK]
    sine = cs_ref[:, DK:2 * DK]

    def rotate(v):
        return v * cosine + pltpu.roll(v, DK // 2, 1) * sine

    ready(0)
    projected = jnp.dot(normed[...], wkv[...], preferred_element_type=F32)
    own[:, 0:DK] = rotate(projected[:, 0:DK]).astype(BF16)
    lanes = own.shape[1] - DK - dv
    own[:, DK:DK + dv] = projected[:, DK:].astype(BF16)
    own[:, DK + dv:] = jnp.ones((toks, lanes), BF16)
    mine = kvbuf.at[pl.ds(al(s * toks, 16), toks)]
    own_copy = pltpu.make_async_copy(own, mine, loc_sem.at[3])
    own_copy.start()
    own_copy.wait()
    kp = {0: start(remote(mine, mine, kp_s.at[0], kp_r.at[0], (d, partner)))}
    kd = {}
    for k in range(1, Z):
        kd[k] = start(remote(mine, mine, kd_s.at[k - 1], kd_r.at[k - 1], (d, fwd(k))))

    ready(1)
    for h in range(HEADS // 2):
        both = jnp.dot(
            normed[...], wq[:, 2 * h * DK:(2 * h + 2) * DK], preferred_element_type=F32
        )
        queries[2 * h] = rotate(both[:, 0:DK]).astype(BF16)
        queries[2 * h + 1] = rotate(both[:, DK:]).astype(BF16)
    phase2(2)

    factor = DK ** (-0.5) * 1.4426950408889634
    for k in range(Z):
        if k > 0:
            kd[k].wait_recv()
            theirs = kvbuf.at[pl.ds(al(src(k) * toks, 16), toks)]
            kp[k] = start(remote(theirs, theirs, kp_s.at[k], kp_r.at[k], (d, partner)))
        kp[k].wait_recv()
        first = k == 0
        base = al(((z + Z - k) % Z) * 2 * toks, 16)

        def head(h, carry):
            keys = kvbuf[pl.ds(base, 2 * toks), 0:DK]
            values = kvbuf[pl.ds(base, 2 * toks), DK:]
            scores = lax.dot_general(
                queries[h], keys, (((1,), (1,)), ((), ())), preferred_element_type=F32
            )
            top = jnp.max(scores, axis=-1, keepdims=True)
            if not first:
                old = peak[h][:, 0:1]
                top = jnp.maximum(old, top)
            weights = jnp.exp2((scores - top) * factor).astype(BF16)
            got = jnp.dot(weights, values, preferred_element_type=F32)
            if not first:
                got = got + attn[h] * jnp.exp2((old - top) * factor)
            attn[h] = got
            peak[h] = jnp.broadcast_to(top, (toks, 128))
            return carry

        lax.fori_loop(0, HEADS, head, 0)
        if k == 0:
            phase3(2)
        if k == 1:
            phase4(2)

    for h in range(HEADS):
        a = attn[h]
        mixed[:, h * dv:(h + 1) * dv] = (a[:, 0:dv] / a[:, dv:dv + 1]).astype(BF16)

    ready(2)

    outs = []
    for n in range(n_tiles):
        cols = slice(n * TILE, (n + 1) * TILE)
        got = jnp.dot(mixed[...], wo[:, cols], preferred_element_type=F32)
        outv[:, cols] = (skip[:, cols].astype(F32) + got).astype(BF16)
    out_copy = pltpu.make_async_copy(outv, out_hbm, out_sem.at[1])
    out_copy.start()
    for cp in sent:
        cp.wait_send()
    skip_out.wait()
    out_copy.wait()


def body(mesh, section_input, conv_gain, conv_weight, conv_bias, attn_gain, q_weight, kv_weight, o_weight):
    D, S = mesh.shape["dp"], mesh.shape["seq"]
    Z = S // 2
    rows, width = section_input.shape
    toks = rows // 2
    R = q_weight.shape[0]
    G = pieces_of(D, R)
    taps = conv_weight.shape[0]
    nq, nkv, hv = q_weight.shape[1], kv_weight.shape[1], R * S
    dv = nkv - DK
    positions = lax.axis_index("seq") * toks + jnp.arange(toks, dtype=jnp.int32)
    half = DK // 2
    freqs = jnp.power(10000.0, -jnp.arange(half, dtype=F32) / half)
    angle = positions.astype(F32)[:, None] * freqs[None, :]
    co, si = jnp.cos(angle), jnp.sin(angle)
    cs = jnp.concatenate([co, co, -si, si], axis=-1)
    anys = pl.BlockSpec(memory_space=pl.ANY)
    vmem = pl.BlockSpec(memory_space=pltpu.VMEM)
    dma = pltpu.SemaphoreType.DMA
    lanes = -(-nkv // 128) * 128
    if lanes == nkv:
        lanes += 128
    z1 = max(Z - 1, 1)
    return pl.pallas_call(
        functools.partial(kernel, (D, S, G, R)),
        out_shape=(
            jax.ShapeDtypeStruct((toks, width), BF16),
            jax.ShapeDtypeStruct((toks, width), BF16),
        ),
        in_specs=[anys, vmem, anys, vmem, vmem, anys, anys, anys, vmem],
        out_specs=(anys, anys),
        scratch_shapes=[
            pltpu.VMEM((rows, width), BF16),
            pltpu.VMEM((2, 16, width), BF16),
            pltpu.VMEM((width // 128, rows, 128), F32),
            pltpu.VMEM((width // 128, rows + 16, 128), F32),
            pltpu.VMEM(((taps + 1) * toks, width), BF16),
            pltpu.VMEM((width // TILE, taps, width, TILE), BF16),
            pltpu.VMEM((rows, TILE), F32),
            pltpu.VMEM((toks, width), BF16),
            pltpu.VMEM((toks, width), BF16),
            pltpu.VMEM((R * S, nq), BF16),
            pltpu.VMEM((R * S, nkv), BF16),
            pltpu.VMEM((R * S, width), BF16),
            pltpu.VMEM((toks, lanes), BF16),
            pltpu.VMEM((S * toks, lanes), BF16),
            pltpu.VMEM((HEADS, toks, DK), BF16),
            pltpu.VMEM((HEADS, toks, 128), F32),
            pltpu.VMEM((HEADS, toks, lanes - DK), F32),
            pltpu.VMEM((toks, hv), BF16),
            pltpu.VMEM((toks, width), BF16),
            dma, dma((width // TILE,)), dma((4,)),
            dma((2,)), dma((2,)),
            dma((3, z1)), dma((3, z1)), dma((3, z1)), dma((3, z1)),
            dma((3, z1, 2)), dma((3, z1, 2)), dma((3, Z)), dma((3, Z)),
            dma((z1,)), dma((z1,)), dma((Z,)), dma((Z,)), dma((2,)),
        ],
        compiler_params=pltpu.CompilerParams(
            collective_id=0, has_side_effects=True, vmem_limit_bytes=66 * 1000 * 1000
        ),
        name="block",
    )(
        section_input, conv_gain[None, :], conv_weight, conv_bias[None, :], attn_gain[None, :],
        q_weight, kv_weight, o_weight, cs,
    )


def solution(mesh):
    row = P(("dp", "seq"), None)
    seq = P("seq", None)
    in_specs = (row, P(), P(), P(), P(), seq, seq, seq)
    return jax.shard_map(
        functools.partial(body, mesh), mesh=mesh, in_specs=in_specs, out_specs=(row, row), check_vma=False
    )
```

time: 161 us -> 95.4 us (0.59); the launches traced: 158 us -> 95.1 us
  Pallas kernels: 0 us -> 85 us
  matrix products: 49.1 us -> 0 us
  waiting for transfers between devices: 47.6 us -> 0 us
  blocking collectives: 20.2 us -> 0 us
  other arithmetic: 20 us -> 1.43 us
  between operations: 14 us -> 0.66 us
  local copies, waits for them, and re-layouts: 1.6 us -> 8 us
  starting transfers between devices: 5.81 us -> 0 us
    pallas_call x0 -> x1, Pallas kernels: none -> 85 us  [body(): pl.pallas_call(functools.partial(kernel, (D, S, G, R)), out_shape=(jax.Sh...]
    dot_general x10 -> x0, matrix products: 49.1 us -> none  [the longest x5 23.6 us: body(): jnp.dot(padded[kernel_tap:kernel_tap + pos_rows], conv_weight[kernel_tap]...]
    all_gather x3 -> x0, waiting for transfers between devices: 46.9 us -> none  [the longest x1 26 us: body(): lax.all_gather(o_weight, 'seq', axis=0, tiled=True)]
    all_gather x1 -> x0, blocking collectives: 20.2 us -> none  [body(): lax.all_gather(kv_weight, 'seq', axis=0, tiled=True)]
    reduce_sum x3 -> x0, other arithmetic: 11.5 us -> none  [the longest x1 9.45 us: body(): total_new = jnp.sum(weights, axis=-1)]
    ppermute x2 -> x0, starting transfers between devices: 5.69 us -> none  [the longest x1 3.77 us: padded_2(): before = lax.ppermute(last, axis, up)]
    reduce_max x1 -> x0, other arithmetic: 4.3 us -> none  [body(): jnp.max(summed.reshape(tok_rows, 2, width), axis=1).astype(jnp.bfloat16)]
    unnamed x15 -> x2, local copies, waits for them, and re-layouts: 0.24 us -> 4.13 us
  transfers between devices with their start and end apart: 5 -> 0, of which waited for: 2 -> 0; matrix products, arithmetic and copies ran while one was open for 39% -> 0% of each run, Pallas kernels for 0% -> 0%
where the time goes in v1:
time: 95.4 us; the launch traced here: 95.1 us
  Pallas kernels  85 us (89%)
  local copies, waits for them, and re-layouts  8 us (8%)
  other arithmetic  1.43 us (1%)
    pallas_call x1, Pallas kernels, body(): pl.pallas_call(functools.partial(kernel, (D, S, G, R)), out_shape=(jax.Sh...  85 us
    unnamed x2, local copies, waits for them, and re-layouts  4.13 us

profile of v1, /device:TPU:17, one launch (start us, length us, event | category | flops | bytes accessed | tf_op | source)
XLA Modules:
  0.0 95.1 jit_solution(14648294193310186984)
XLA Ops:
  0.7 1.3 %broadcast_in_dim.11.cgain = f32[1,1536]{1,0:T(1,128)} reshape(f32[1536]{0:T(1024)} %param.9) | data formatting | bytes 12288 | tf_op jit(solution)/shard_map/broadcast_in_dim | solution.py:368
  2.0 1.3 %broadcast_in_dim.12.cbias = f32[1,1536]{1,0:T(1,128)} reshape(f32[1536]{0:T(1024)} %param.11) | data formatting | bytes 12288 | tf_op jit(solution)/shard_map/broadcast_in_dim | solution.py:368
  3.2 1.3 %broadcast_in_dim.13.again = f32[1,1536]{1,0:T(1,128)} reshape(f32[1536]{0:T(1024)} %param.12) | data formatting | bytes 12288 | tf_op jit(solution)/shard_map/broadcast_in_dim | solution.py:368
  4.5 0.5 multiply_cosine_fusion
  5.1 0.9 pad_maximum_fusion.cs_ref
  6.0 85.0 %block.1 = (bf16[256,1536]{1,0:T(8,128)(2,1)}, bf16[256,1536]{1,0:T(8,128)(2,1)}) custom-call(bf16[512,1536]{1,0:T(8,128)(2,1)} %x_hbm.1, f32[1,1536]{1,0:T(1,128)} %broadcast_in_dim.11.cgain, bf16[5,1536,1536]{2,1,0:T(8,128)(2,1)} %cw_hbm.1, f32[1,1536]{1,0:T(1,128)} %broadcast_in_dim.12.cbias, f32[1,1536]{1,0:T(1,128)} %broadcast_in_dim.13.again, ...), custom_call_target="tpu_custom_call" | custom-call | tf_op jit(solution)/shard_map/block/pallas_call | solution.py:329
  90.9 2.1 %copy.13 = bf16[256,1536]{1,0:T(8,128)(2,1)} copy(bf16[256,1536]{1,0:T(8,128)(2,1)} %get-tuple-element.7) | data formatting | bytes 1572864
  93.0 2.1 %copy.14 = bf16[256,1536]{1,0:T(8,128)(2,1)} copy(bf16[256,1536]{1,0:T(8,128)(2,1)} %get-tuple-element.8) | data formatting | bytes 1572864
  (2 shorter events, 0.0 us)

commit v2 on v1

--- a/solution.py
+++ b/solution.py
@@ -10,6 +10,7 @@
 HEADS = 8
 DK = 128
 TILE = 256
+UNROLL = 4
 F32 = jnp.float32
 BF16 = jnp.bfloat16
 MESH = pl.DeviceIdType.MESH
@@ -23,10 +24,10 @@
 
 
 def kernel(
-    cfg, x_hbm, cgain, cw_hbm, cbias, again, q_hbm, kv_hbm, o_hbm, cs_ref,
+    cfg, x_hbm, cgain, cw_hbm, cbias, again, q_hbm, kv_hbm, o_hbm, cos_ref, sin_ref,
     skip_hbm, out_hbm,
-    xin, halo, resid, pad, stack, cw, acc, skip, normed, wq, wkv, wo, own, kvbuf, queries,
-    peak, attn, mixed, outv,
+    xin, halo, resid, pad, stack, cw, acc, skip, normed, wq, wkv, wo, own_k, own_v, kbuf, vbuf, queries,
+    peak, attn, mixed, outv, vecs,
     in_sem, cw_sem, loc_sem, halo_s, halo_r, p1_s, p1_r, p2_s, p2_r, p3_s, p3_r, p4_s, p4_r,
     kd_s, kd_r, kp_s, kp_r, out_sem,
 ):
@@ -155,9 +156,12 @@
     phase1(0)
     phase1(1)
 
+    for i, vec in enumerate((cgain, cbias, again)):
+        vecs[i:i + 1, :] = vec[...].reshape(1, width)
+
     def act(v):
         scale = lax.rsqrt(jnp.mean(v * v, axis=-1, keepdims=True) + 1e-06)
-        return jax.nn.gelu(v * scale * cgain[...], approximate=True)
+        return jax.nn.gelu(v * scale * vecs[0:1, :], approximate=True)
 
     in_copy.wait()
     step_rows = 16
@@ -190,7 +194,7 @@
               4: (lambda: phase4(0), lambda: phase4(1))}
     for n in range(n_tiles):
         cw_copies[n].wait()
-        acc[...] = jnp.broadcast_to(cbias[:, n * TILE:(n + 1) * TILE], acc.shape)
+        acc[...] = jnp.broadcast_to(vecs[1:2, n * TILE:(n + 1) * TILE], acc.shape)
 
         def tap(t, carry):
             acc[...] += jnp.dot(
@@ -215,31 +219,36 @@
         at = pl.ds(al(i * 16, 16), 16)
         v = skip[at, :].astype(F32)
         scale = lax.rsqrt(jnp.mean(v * v, axis=-1, keepdims=True) + 1e-06)
-        normed[at, :] = (v * scale * again[...]).astype(BF16)
+        normed[at, :] = (v * scale * vecs[2:3, :]).astype(BF16)
         return carry
 
     lax.fori_loop(0, toks // 16, norm_rows, 0)
 
-    cosine = cs_ref[:, 0:DK]
-    sine = cs_ref[:, DK:2 * DK]
+    cosine = cos_ref[...]
+    sine = sin_ref[...]
 
     def rotate(v):
         return v * cosine + pltpu.roll(v, DK // 2, 1) * sine
 
     ready(0)
     projected = jnp.dot(normed[...], wkv[...], preferred_element_type=F32)
-    own[:, 0:DK] = rotate(projected[:, 0:DK]).astype(BF16)
-    lanes = own.shape[1] - DK - dv
-    own[:, DK:DK + dv] = projected[:, DK:].astype(BF16)
-    own[:, DK + dv:] = jnp.ones((toks, lanes), BF16)
-    mine = kvbuf.at[pl.ds(al(s * toks, 16), toks)]
-    own_copy = pltpu.make_async_copy(own, mine, loc_sem.at[3])
-    own_copy.start()
-    own_copy.wait()
-    kp = {0: start(remote(mine, mine, kp_s.at[0], kp_r.at[0], (d, partner)))}
-    kd = {}
+    own_k[...] = rotate(projected[:, 0:DK]).astype(BF16)
+    own_v[0:dv, :] = jnp.transpose(projected[:, DK:]).astype(BF16)
+    own_v[dv:, :] = jnp.ones((own_v.shape[0] - dv, toks), BF16)
+    mine = (kbuf.at[s], vbuf.at[s])
+    own_copies = []
+    for i, (a, b) in enumerate(zip((own_k, own_v), mine)):
+        cp = pltpu.make_async_copy(a, b, loc_sem.at[3 + i])
+        cp.start()
+        own_copies.append(cp)
+    for cp in own_copies:
+        cp.wait()
+    kp, kd = {}, {}
+    for i, a in enumerate(mine):
+        kp[0, i] = start(remote(a, a, kp_s.at[i, 0], kp_r.at[i, 0], (d, partner)))
     for k in range(1, Z):
-        kd[k] = start(remote(mine, mine, kd_s.at[k - 1], kd_r.at[k - 1], (d, fwd(k))))
+        for i, a in enumerate(mine):
+            kd[k, i] = start(remote(a, a, kd_s.at[i, k - 1], kd_r.at[i, k - 1], (d, fwd(k))))
 
     ready(1)
     for h in range(HEADS // 2):
@@ -252,33 +261,43 @@
 
     factor = DK ** (-0.5) * 1.4426950408889634
     for k in range(Z):
-        if k > 0:
-            kd[k].wait_recv()
-            theirs = kvbuf.at[pl.ds(al(src(k) * toks, 16), toks)]
-            kp[k] = start(remote(theirs, theirs, kp_s.at[k], kp_r.at[k], (d, partner)))
-        kp[k].wait_recv()
+        for i, buf in enumerate((kbuf, vbuf)):
+            if k > 0:
+                kd[k, i].wait_recv()
+                at = buf.at[src(k)]
+                kp[k, i] = start(remote(at, at, kp_s.at[i, k], kp_r.at[i, k], (d, partner)))
+        for i in range(2):
+            kp[k, i].wait_recv()
         first = k == 0
-        base = al(((z + Z - k) % Z) * 2 * toks, 16)
-
-        def head(h, carry):
-            keys = kvbuf[pl.ds(base, 2 * toks), 0:DK]
-            values = kvbuf[pl.ds(base, 2 * toks), DK:]
-            scores = lax.dot_general(
-                queries[h], keys, (((1,), (1,)), ((), ())), preferred_element_type=F32
-            )
-            top = jnp.max(scores, axis=-1, keepdims=True)
+        base = ((z + Z - k) % Z) * 2
+
+        def head(h):
+            scores = [
+                lax.dot_general(
+                    kbuf[base + j], queries[h], (((1,), (1,)), ((), ())), preferred_element_type=F32
+                )
+                for j in range(2)
+            ]
+            top = jnp.max(jnp.maximum(scores[0], scores[1]), axis=0, keepdims=True)
             if not first:
-                old = peak[h][:, 0:1]
+                old = peak[h][0:1, :]
                 top = jnp.maximum(old, top)
-            weights = jnp.exp2((scores - top) * factor).astype(BF16)
-            got = jnp.dot(weights, values, preferred_element_type=F32)
+            got = None
+            for j in range(2):
+                weights = jnp.exp2((scores[j] - top) * factor).astype(BF16)
+                part = jnp.dot(vbuf[base + j], weights, preferred_element_type=F32)
+                got = part if got is None else got + part
             if not first:
                 got = got + attn[h] * jnp.exp2((old - top) * factor)
             attn[h] = got
-            peak[h] = jnp.broadcast_to(top, (toks, 128))
+            peak[h] = jnp.broadcast_to(top, (8, toks))
+
+        def heads(i, carry):
+            for u in range(UNROLL):
+                head(i * UNROLL + u)
             return carry
 
-        lax.fori_loop(0, HEADS, head, 0)
+        lax.fori_loop(0, HEADS // UNROLL, heads, 0)
         if k == 0:
             phase3(2)
         if k == 1:
@@ -286,7 +305,7 @@
 
     for h in range(HEADS):
         a = attn[h]
-        mixed[:, h * dv:(h + 1) * dv] = (a[:, 0:dv] / a[:, dv:dv + 1]).astype(BF16)
+        mixed[:, h * dv:(h + 1) * dv] = jnp.transpose(a[0:dv, :] / a[dv:dv + 1, :]).astype(BF16)
 
     ready(2)
 
@@ -315,16 +334,13 @@
     dv = nkv - DK
     positions = lax.axis_index("seq") * toks + jnp.arange(toks, dtype=jnp.int32)
     half = DK // 2
-    freqs = jnp.power(10000.0, -jnp.arange(half, dtype=F32) / half)
+    freqs = jnp.power(10000.0, -(jnp.arange(DK, dtype=jnp.int32) % half).astype(F32) / half)
     angle = positions.astype(F32)[:, None] * freqs[None, :]
-    co, si = jnp.cos(angle), jnp.sin(angle)
-    cs = jnp.concatenate([co, co, -si, si], axis=-1)
+    cosine = jnp.cos(angle)
+    sine = jnp.sin(angle) * jnp.where(jnp.arange(DK) < half, -1.0, 1.0).astype(F32)
     anys = pl.BlockSpec(memory_space=pl.ANY)
     vmem = pl.BlockSpec(memory_space=pltpu.VMEM)
     dma = pltpu.SemaphoreType.DMA
-    lanes = -(-nkv // 128) * 128
-    if lanes == nkv:
-        lanes += 128
     z1 = max(Z - 1, 1)
     return pl.pallas_call(
         functools.partial(kernel, (D, S, G, R)),
@@ -332,7 +348,7 @@
             jax.ShapeDtypeStruct((toks, width), BF16),
             jax.ShapeDtypeStruct((toks, width), BF16),
         ),
-        in_specs=[anys, vmem, anys, vmem, vmem, anys, anys, anys, vmem],
+        in_specs=[anys, vmem, anys, vmem, vmem, anys, anys, anys, vmem, vmem],
         out_specs=(anys, anys),
         scratch_shapes=[
             pltpu.VMEM((rows, width), BF16),
@@ -347,26 +363,29 @@
             pltpu.VMEM((R * S, nq), BF16),
             pltpu.VMEM((R * S, nkv), BF16),
             pltpu.VMEM((R * S, width), BF16),
-            pltpu.VMEM((toks, lanes), BF16),
-            pltpu.VMEM((S * toks, lanes), BF16),
+            pltpu.VMEM((toks, DK), BF16),
+            pltpu.VMEM((dv + 16, toks), BF16),
+            pltpu.VMEM((S, toks, DK), BF16),
+            pltpu.VMEM((S, dv + 16, toks), BF16),
             pltpu.VMEM((HEADS, toks, DK), BF16),
-            pltpu.VMEM((HEADS, toks, 128), F32),
-            pltpu.VMEM((HEADS, toks, lanes - DK), F32),
+            pltpu.VMEM((HEADS, 8, toks), F32),
+            pltpu.VMEM((HEADS, dv + 16, toks), F32),
             pltpu.VMEM((toks, hv), BF16),
             pltpu.VMEM((toks, width), BF16),
-            dma, dma((width // TILE,)), dma((4,)),
+            pltpu.VMEM((8, width), F32),
+            dma, dma((width // TILE,)), dma((5,)),
             dma((2,)), dma((2,)),
             dma((3, z1)), dma((3, z1)), dma((3, z1)), dma((3, z1)),
             dma((3, z1, 2)), dma((3, z1, 2)), dma((3, Z)), dma((3, Z)),
-            dma((z1,)), dma((z1,)), dma((Z,)), dma((Z,)), dma((2,)),
+            dma((2, z1)), dma((2, z1)), dma((2, Z)), dma((2, Z)), dma((2,)),
         ],
         compiler_params=pltpu.CompilerParams(
-            collective_id=0, has_side_effects=True, vmem_limit_bytes=66 * 1000 * 1000
+            collective_id=0, vmem_limit_bytes=66 * 1000 * 1000
         ),
         name="block",
     )(
-        section_input, conv_gain[None, :], conv_weight, conv_bias[None, :], attn_gain[None, :],
-        q_weight, kv_weight, o_weight, cs,
+        section_input, conv_gain, conv_weight, conv_bias, attn_gain, q_weight, kv_weight, o_weight,
+        cosine, sine,
     )
 
 

time: 95.4 us -> 80.7 us (0.85)
  Pallas kernels: 85 us -> 74.1 us
  local copies, waits for them, and re-layouts: 8 us -> 4.13 us
    pallas_call x1, Pallas kernels: 85 us -> 74.1 us  [body(): pl.pallas_call(functools.partial(kernel, (D, S, G, R)), out_shape=(jax.Sh...]
    broadcast_in_dim x3 -> x0, local copies, waits for them, and re-layouts: 3.88 us -> none  [the longest x1 1.3 us: body(): conv_gain[None, :]]
    mul x0 -> x1, other arithmetic: none -> 1.24 us  [body(): jnp.sin(angle) * jnp.where(jnp.arange(DK) < half, -1.0, 1.0).astype(F32)]
where the time goes in v2:
time: 80.7 us; the launch traced here: 80.1 us
  Pallas kernels  74.1 us (92%)
  local copies, waits for them, and re-layouts  4.13 us (5%)
  other arithmetic  1.25 us (2%)
    pallas_call x1, Pallas kernels, body(): pl.pallas_call(functools.partial(kernel, (D, S, G, R)), out_shape=(jax.Sh...  74.1 us
    unnamed x2, local copies, waits for them, and re-layouts  4.13 us

profile of v2, /device:TPU:17, one launch (start us, length us, event | category | flops | bytes accessed | tf_op | source)
XLA Modules:
  0.0 80.1 jit_solution(16223137720530455579)
XLA Ops:
  0.7 1.2 %fusion = (f32[256,128]{1,0:T(8,128)}, f32[256,128]{1,0:T(8,128)}) fusion(f32[128]{0:T(128)S(1)} %get-tuple-element.4, f32[128]{0:T(128)S(1)} %get-tuple-element.5, f32[256]{0:T(256)S(1)} %add_convert_fusion), kind=kLoop, calls=%fused_computation.2 | loop fusion | flops 65536 | bytes 264192 | tf_op jit(solution)/shard_map/mul | solution.py:340
  1.9 74.1 %block.1 = (bf16[256,1536]{1,0:T(8,128)(2,1)}, bf16[256,1536]{1,0:T(8,128)(2,1)}) custom-call(bf16[512,1536]{1,0:T(8,128)(2,1)} %x_hbm.1, f32[1536]{0:T(1024)} %cgain.1, bf16[5,1536,1536]{2,1,0:T(8,128)(2,1)} %cw_hbm.1, f32[1536]{0:T(1024)} %cbias.1, f32[1536]{0:T(1024)} %again.1, bf16[192,1024]{1,0:T(8,128)(2,1)} %q_hbm.1, bf16[192,320]{1,0:T(8,128)(2,1)} %kv_hbm.1, ...), custom_call_target="tpu_custom_call" | custom-call | tf_op jit(solution)/shard_map/block/pallas_call | solution.py:345
  76.0 2.1 %copy.12 = bf16[256,1536]{1,0:T(8,128)(2,1)} copy(bf16[256,1536]{1,0:T(8,128)(2,1)} %get-tuple-element.8) | data formatting | bytes 1572864
  78.0 2.1 %copy.13 = bf16[256,1536]{1,0:T(8,128)(2,1)} copy(bf16[256,1536]{1,0:T(8,128)(2,1)} %get-tuple-element.9) | data formatting | bytes 1572864
  (2 shorter events, 0.0 us)

commit v3 on v2

--- a/solution.py
+++ b/solution.py
@@ -25,11 +25,11 @@
 
 def kernel(
     cfg, x_hbm, cgain, cw_hbm, cbias, again, q_hbm, kv_hbm, o_hbm, cos_ref, sin_ref,
-    skip_hbm, out_hbm,
-    xin, halo, resid, pad, stack, cw, acc, skip, normed, wq, wkv, wo, own_k, own_v, kbuf, vbuf, queries,
-    peak, attn, mixed, outv, vecs,
+    skip, outv,
+    xin, halo, resid, pad, stack, cw, acc, normed, wq, wkv, wo, own_k, own_v, kbuf, vbuf, queries,
+    peak, attn, mixed, vecs,
     in_sem, cw_sem, loc_sem, halo_s, halo_r, p1_s, p1_r, p2_s, p2_r, p3_s, p3_r, p4_s, p4_r,
-    kd_s, kd_r, kp_s, kp_r, out_sem,
+    kd_s, kd_r, kp_s, kp_r,
 ):
     D, S, G, R = cfg
     Z = S // 2
@@ -212,8 +212,6 @@
         for e in events.get(n, ()):
             e()
 
-    skip_out = pltpu.make_async_copy(skip, skip_hbm, out_sem.at[0])
-    skip_out.start()
 
     def norm_rows(i, carry):
         at = pl.ds(al(i * 16, 16), 16)
@@ -314,12 +312,8 @@
         cols = slice(n * TILE, (n + 1) * TILE)
         got = jnp.dot(mixed[...], wo[:, cols], preferred_element_type=F32)
         outv[:, cols] = (skip[:, cols].astype(F32) + got).astype(BF16)
-    out_copy = pltpu.make_async_copy(outv, out_hbm, out_sem.at[1])
-    out_copy.start()
     for cp in sent:
         cp.wait_send()
-    skip_out.wait()
-    out_copy.wait()
 
 
 def body(mesh, section_input, conv_gain, conv_weight, conv_bias, attn_gain, q_weight, kv_weight, o_weight):
@@ -345,11 +339,11 @@
     return pl.pallas_call(
         functools.partial(kernel, (D, S, G, R)),
         out_shape=(
-            jax.ShapeDtypeStruct((toks, width), BF16),
-            jax.ShapeDtypeStruct((toks, width), BF16),
+            pltpu.VMEM((toks, width), BF16),
+            pltpu.VMEM((toks, width), BF16),
         ),
         in_specs=[anys, vmem, anys, vmem, vmem, anys, anys, anys, vmem, vmem],
-        out_specs=(anys, anys),
+        out_specs=(vmem, vmem),
         scratch_shapes=[
             pltpu.VMEM((rows, width), BF16),
             pltpu.VMEM((2, 16, width), BF16),
@@ -358,7 +352,6 @@
             pltpu.VMEM(((taps + 1) * toks, width), BF16),
             pltpu.VMEM((width // TILE, taps, width, TILE), BF16),
             pltpu.VMEM((rows, TILE), F32),
-            pltpu.VMEM((toks, width), BF16),
             pltpu.VMEM((toks, width), BF16),
             pltpu.VMEM((R * S, nq), BF16),
             pltpu.VMEM((R * S, nkv), BF16),
@@ -371,16 +364,15 @@
             pltpu.VMEM((HEADS, 8, toks), F32),
             pltpu.VMEM((HEADS, dv + 16, toks), F32),
             pltpu.VMEM((toks, hv), BF16),
-            pltpu.VMEM((toks, width), BF16),
             pltpu.VMEM((8, width), F32),
             dma, dma((width // TILE,)), dma((5,)),
             dma((2,)), dma((2,)),
             dma((3, z1)), dma((3, z1)), dma((3, z1)), dma((3, z1)),
             dma((3, z1, 2)), dma((3, z1, 2)), dma((3, Z)), dma((3, Z)),
-            dma((2, z1)), dma((2, z1)), dma((2, Z)), dma((2, Z)), dma((2,)),
+            dma((2, z1)), dma((2, z1)), dma((2, Z)), dma((2, Z)),
         ],
         compiler_params=pltpu.CompilerParams(
-            collective_id=0, vmem_limit_bytes=66 * 1000 * 1000
+            collective_id=0, vmem_limit_bytes=58 * 1000 * 1000
         ),
         name="block",
     )(

time: 80.7 us -> 77.5 us (0.960)
  local copies, waits for them, and re-layouts: 4.13 us -> 1.76 us
    unnamed x2, local copies, waits for them, and re-layouts: 4.13 us -> 1.76 us
where the time goes in v3:
time: 77.5 us; the launch traced here: 77 us
  Pallas kernels  73.3 us (95%)
  local copies, waits for them, and re-layouts  1.76 us (2%)
  other arithmetic  1.25 us (2%)
    pallas_call x1, Pallas kernels, body(): pl.pallas_call(functools.partial(kernel, (D, S, G, R)), out_shape=(pltpu....  73.3 us
    unnamed x2, local copies, waits for them, and re-layouts  1.76 us

profile of v3, /device:TPU:17, one launch (start us, length us, event | category | flops | bytes accessed | tf_op | source)
XLA Modules:
  0.0 77.0 jit_solution(15193908838765414704)
XLA Ops:
  0.7 1.2 %fusion = (f32[256,128]{1,0:T(8,128)}, f32[256,128]{1,0:T(8,128)}) fusion(f32[128]{0:T(128)S(1)} %get-tuple-element.4, f32[128]{0:T(128)S(1)} %get-tuple-element.5, f32[256]{0:T(256)S(1)} %add_convert_fusion), kind=kLoop, calls=%fused_computation.2 | loop fusion | flops 65536 | bytes 264192 | tf_op jit(solution)/shard_map/mul | solution.py:334
  1.9 73.3 %block.1 = (bf16[256,1536]{1,0:T(8,128)(2,1)S(1)}, bf16[256,1536]{1,0:T(8,128)(2,1)S(1)}) custom-call(bf16[512,1536]{1,0:T(8,128)(2,1)} %x_hbm.1, f32[1536]{0:T(1024)} %cgain.1, bf16[5,1536,1536]{2,1,0:T(8,128)(2,1)} %cw_hbm.1, f32[1536]{0:T(1024)} %cbias.1, f32[1536]{0:T(1024)} %again.1, bf16[192,1024]{1,0:T(8,128)(2,1)} %q_hbm.1, bf16[192,320]{1,0:T(8,128)(2,1)} %kv_hbm.1, ...), custom_call_target="tpu_custom_call" | custom-call | tf_op jit(solution)/shard_map/block/pallas_call | solution.py:339
  75.2 0.9 %copy.12 = bf16[256,1536]{1,0:T(8,128)(2,1)} copy(bf16[256,1536]{1,0:T(8,128)(2,1)S(1)} %get-tuple-element.6) | data formatting | bytes 1572864
  76.1 0.9 %copy.13 = bf16[256,1536]{1,0:T(8,128)(2,1)} copy(bf16[256,1536]{1,0:T(8,128)(2,1)S(1)} %get-tuple-element.7) | data formatting | bytes 1572864
  (2 shorter events, 0.0 us)

commit v4 on v3

--- a/solution.py
+++ b/solution.py
@@ -72,7 +72,8 @@
         cp = pltpu.make_async_copy(
             cw_hbm.at[:, :, pl.ds(n * TILE, TILE)], cw.at[n], cw_sem.at[n]
         )
-        cp.start()
+        if n < 2:
+            cp.start()
         cw_copies.append(cp)
 
     greet = [(d, up), (d, down), (d, partner)] + [(d, fwd(k)) for k in range(1, Z)]
@@ -189,11 +190,13 @@
                 j, pl.ds(6 + b, toks, stride=2), :
             ].astype(BF16)
 
-    events = {1: (lambda: phase2(0), lambda: phase2(1), lambda: phase1(2)),
-              3: (lambda: phase3(0), lambda: phase3(1)),
-              4: (lambda: phase4(0), lambda: phase4(1))}
+    events = {0: (lambda: phase2(0), lambda: phase2(1)),
+              2: (lambda: phase3(0), lambda: phase3(1), lambda: phase1(2)),
+              4: (lambda: phase4(0), lambda: phase4(1), lambda: phase2(2))}
     for n in range(n_tiles):
         cw_copies[n].wait()
+        if n + 2 < n_tiles:
+            cw_copies[n + 2].start()
         acc[...] = jnp.broadcast_to(vecs[1:2, n * TILE:(n + 1) * TILE], acc.shape)
 
         def tap(t, carry):
@@ -255,7 +258,6 @@
         )
         queries[2 * h] = rotate(both[:, 0:DK]).astype(BF16)
         queries[2 * h + 1] = rotate(both[:, DK:]).astype(BF16)
-    phase2(2)
 
     factor = DK ** (-0.5) * 1.4426950408889634
     for k in range(Z):

time: 77.5 us -> 74.8 us (0.965)
  Pallas kernels: 73.3 us -> 70.5 us
    pallas_call x1, Pallas kernels: 73.3 us -> 70.5 us  [body(): pl.pallas_call(functools.partial(kernel, (D, S, G, R)), out_shape=(pltpu....]
where the time goes in v4:
time: 74.8 us; the launch traced here: 74.1 us
  Pallas kernels  70.5 us (94%)
  local copies, waits for them, and re-layouts  1.76 us (2%)
  other arithmetic  1.25 us (2%)
    pallas_call x1, Pallas kernels, body(): pl.pallas_call(functools.partial(kernel, (D, S, G, R)), out_shape=(pltpu....  70.5 us
    unnamed x2, local copies, waits for them, and re-layouts  1.76 us

profile of v4, /device:TPU:17, one launch (start us, length us, event | category | flops | bytes accessed | tf_op | source)
XLA Modules:
  0.0 74.1 jit_solution(2531149732327899570)
XLA Ops:
  0.7 1.2 %fusion = (f32[256,128]{1,0:T(8,128)}, f32[256,128]{1,0:T(8,128)}) fusion(f32[128]{0:T(128)S(1)} %get-tuple-element.4, f32[128]{0:T(128)S(1)} %get-tuple-element.5, f32[256]{0:T(256)S(1)} %add_convert_fusion), kind=kLoop, calls=%fused_computation.2 | loop fusion | flops 65536 | bytes 264192 | tf_op jit(solution)/shard_map/mul | solution.py:336
  1.9 70.5 %block.1 = (bf16[256,1536]{1,0:T(8,128)(2,1)S(1)}, bf16[256,1536]{1,0:T(8,128)(2,1)S(1)}) custom-call(bf16[512,1536]{1,0:T(8,128)(2,1)} %x_hbm.1, f32[1536]{0:T(1024)} %cgain.1, bf16[5,1536,1536]{2,1,0:T(8,128)(2,1)} %cw_hbm.1, f32[1536]{0:T(1024)} %cbias.1, f32[1536]{0:T(1024)} %again.1, bf16[192,1024]{1,0:T(8,128)(2,1)} %q_hbm.1, bf16[192,320]{1,0:T(8,128)(2,1)} %kv_hbm.1, ...), custom_call_target="tpu_custom_call" | custom-call | tf_op jit(solution)/shard_map/block/pallas_call | solution.py:341
  72.4 0.9 %copy.12 = bf16[256,1536]{1,0:T(8,128)(2,1)} copy(bf16[256,1536]{1,0:T(8,128)(2,1)S(1)} %get-tuple-element.6) | data formatting | bytes 1572864
  73.3 0.9 %copy.13 = bf16[256,1536]{1,0:T(8,128)(2,1)} copy(bf16[256,1536]{1,0:T(8,128)(2,1)S(1)} %get-tuple-element.7) | data formatting | bytes 1572864
  (2 shorter events, 0.0 us)
